TPU v7x, 32 devices: a whole 2x2x4 slice. The times are simulated.
32 devices in a mesh: dp: 8 (over z, core), ctx: 4 (over y, x).
Axes of the slice: x: 2, y: 2, z: 4, core: 2. Of those that a mesh axis runs over, the one named last changes fastest.
Arguments:
- hidden_in: bfloat16 [8, 2048, 2048], P('dp', 'ctx'), may hold values from -6 to 6
- ln_gain: bfloat16 [2048], P(('dp', 'ctx')), may hold values from 0.099609375 to 1.8984375
- ln_bias: bfloat16 [2048], P(('dp', 'ctx')), may hold values from -4 to 4
- w_qkv: bfloat16 [2048, 6144], P(('dp', 'ctx')), may hold values from -0.125 to 0.125
- b_qkv: bfloat16 [6144], P(('dp', 'ctx')), may hold values from -4 to 4
- w_out: bfloat16 [2048, 2048], P(('dp', 'ctx')), may hold values from -2 to 2
- b_out: bfloat16 [2048], P(('dp', 'ctx')), may hold values from -4 to 4
- w_up: bfloat16 [2048, 8192], P(('dp', 'ctx')), may hold values from -0.125 to 0.125
- b_up: bfloat16 [8192], P(('dp', 'ctx')), may hold values from -4 to 4
- w_down: bfloat16 [8192, 2048], P(('dp', 'ctx')), may hold values from -0.0625 to 0.0625
- b_down: bfloat16 [2048], P(('dp', 'ctx')), may hold values from -4 to 4
- segment_ids: int32 [8, 2048], P('dp'), may hold values from 0 to 3, as said below
- positions: int32 [8, 2048], P('dp', 'ctx'), may hold values from 0 to 1023, as said below
- token_order: int32 [8, 2048], P('dp'), may hold values from 0 to 2047, as said below
- grad_out: bfloat16 [8, 2048, 2048], P('dp', 'ctx'), may hold values from -6 to 6
Outputs:
- output: bfloat16 [8, 2048, 2048], P('dp', 'ctx')
- grad_in: bfloat16 [8, 2048, 2048], P('dp', 'ctx')
- grad_ln_gain: float32 [2048], P(('dp', 'ctx'))
- grad_ln_bias: float32 [2048], P(('dp', 'ctx'))
- grad_w_qkv: float32 [2048, 6144], P(('dp', 'ctx'))
- grad_b_qkv: float32 [6144], P(('dp', 'ctx'))
- grad_w_out: float32 [2048, 2048], P(('dp', 'ctx'))
- grad_b_out: float32 [2048], P(('dp', 'ctx'))
- grad_w_up: float32 [2048, 8192], P(('dp', 'ctx'))
- grad_b_up: float32 [8192], P(('dp', 'ctx'))
- grad_w_down: float32 [8192, 2048], P(('dp', 'ctx'))
- grad_b_down: float32 [2048], P(('dp', 'ctx'))
Inputs may be any that keep to these rules, and one draw needn't show every extreme that they name: Each row's places 0 to 2047 form 4 documents of consecutive places, numbered in order of place, one of which holds exactly 1024 places; segment_ids gives the document of the place token_order assigns to each slot. `positions`: A slot's place minus the first place of its document. `token_order`: each row is a permutation of its places that moves whole runs of 128 places: slots 128 b to 128 b + 127 hold the places of one run in rising order.
All inputs are finite; a program needn't handle non-finite values.
Results may differ from a plain program's by a relative error of at most 0.0095.
Values may be sent and summed in bfloat16 or wider, within the bound.
No kernel may reach another device: no remote copies, remote signals or barrier semaphores. Data moves between devices by JAX's collectives and lax.ppermute only.
A program may use at most 512 MiB of HBM per device.

v0:
```python
import math
import jax
import jax.numpy as jnp
from jax import lax
from jax.sharding import PartitionSpec as P

HEAD = 64
ROT = 32
EPS = 1e-05
NEG = -1e30


def norm_rows(values, gain, shift):
    average = jnp.mean(values, axis=-1, keepdims=True)
    centred = values - average
    variance = jnp.mean(centred * centred, axis=-1, keepdims=True)
    return centred * lax.rsqrt(variance + EPS) * gain + shift


def angle_table(position_rows):
    half_width = ROT // 2
    frequency = 10000.0 ** (-jnp.arange(half_width, dtype=jnp.float32) * 2.0 / ROT)
    angles = position_rows.astype(jnp.float32)[..., None] * frequency
    return (jnp.cos(angles)[..., None, :], jnp.sin(angles)[..., None, :])


def rotate(values, cosine, sine_table):
    half_width = cosine.shape[-1]
    front_part = values[..., :half_width]
    back_part = values[..., half_width : 2 * half_width]
    return jnp.concatenate(
        [
            front_part * cosine - back_part * sine_table,
            back_part * cosine + front_part * sine_table,
            values[..., 2 * half_width :],
        ],
        axis=-1,
    )


def unrotate(gradient, cosine, sine_table):
    half_width = cosine.shape[-1]
    front_part = gradient[..., :half_width]
    back_part = gradient[..., half_width : 2 * half_width]
    return jnp.concatenate(
        [
            front_part * cosine + back_part * sine_table,
            back_part * cosine - front_part * sine_table,
            gradient[..., 2 * half_width :],
        ],
        axis=-1,
    )


def head_groups(tensor, group_size):
    row_count, slot_count, head_count, head_width = tensor.shape
    shaped = tensor.reshape(row_count, slot_count, head_count // group_size, group_size, head_width)
    return jnp.moveaxis(shaped, 2, 0)


def join_groups(tensor):
    group_count, row_count, slot_count, group_size, head_width = tensor.shape
    return jnp.moveaxis(tensor, 0, 2).reshape(
        row_count, slot_count, group_count * group_size, head_width
    )


def masked_scores(q_group, k_group, allowed, score_scale):
    scores = (
        jnp.einsum("btge,blge->bgtl", q_group, k_group, preferred_element_type=jnp.float32)
        * score_scale
    )
    return jnp.where(allowed[:, None], scores, NEG)


def attend(queries, keys_all, values_all, allowed, score_scale):

    def one_group(pieces):
        q_group, k_group, v_group = pieces
        scores = masked_scores(q_group, k_group, allowed, score_scale)
        row_top = jnp.max(scores, axis=-1, keepdims=True)
        weights = jnp.exp(scores - row_top)
        totals = jnp.sum(weights, axis=-1, keepdims=True)
        probabilities = (weights / totals).astype(jnp.bfloat16)
        mixed_out = jnp.einsum(
            "bgtl,blge->btge", probabilities, v_group, preferred_element_type=jnp.float32
        )
        return (mixed_out.astype(jnp.bfloat16), (row_top + jnp.log(totals))[..., 0])

    return lax.map(one_group, (queries, keys_all, values_all))


def attend_back(queries, keys_all, values_all, d_attended, log_totals, allowed, score_scale):

    def one_group(pieces):
        q_group, k_group, v_group, d_group, l_group = pieces
        scores = masked_scores(q_group, k_group, allowed, score_scale)
        probs_full = jnp.exp(scores - l_group[..., None])
        probs_low = probs_full.astype(jnp.bfloat16)
        d_probs = jnp.einsum(
            "btge,blge->bgtl", d_group, v_group, preferred_element_type=jnp.float32
        )
        inner_sum = jnp.sum(probs_full * d_probs, axis=-1, keepdims=True)
        d_scores = (probs_full * (d_probs - inner_sum)).astype(jnp.bfloat16)
        d_query = (
            jnp.einsum("bgtl,blge->btge", d_scores, k_group, preferred_element_type=jnp.float32)
            * score_scale
        )
        d_key = (
            jnp.einsum("bgtl,btge->blge", d_scores, q_group, preferred_element_type=jnp.float32)
            * score_scale
        )
        d_value = jnp.einsum(
            "bgtl,btge->blge", probs_low, d_group, preferred_element_type=jnp.float32
        )
        return (d_query, d_key, d_value)

    return lax.map(one_group, (queries, keys_all, values_all, d_attended, log_totals))


def run_forward(weights, hidden_in, positions, segment_ids, token_order, fetch):
    w_qkv, w_out, w_up, w_down, b_qkv, b_out, b_up, b_down, ln_gain, ln_bias = weights
    row_count, slot_count, feature = hidden_in.shape
    head_count = feature // HEAD
    group_size = math.gcd(head_count, 4)
    hidden_f = hidden_in.astype(jnp.float32)
    normed = norm_rows(hidden_f, ln_gain.astype(jnp.float32), ln_bias.astype(jnp.float32)).astype(
        jnp.bfloat16
    )
    qkv = jnp.einsum(
        "btd,df->btf", normed, w_qkv, preferred_element_type=jnp.float32
    ) + b_qkv.astype(jnp.float32)
    cosine, sine_table = angle_table(positions)
    queries = rotate(
        qkv[..., :feature].reshape(row_count, slot_count, head_count, HEAD), cosine, sine_table
    ).astype(jnp.bfloat16)
    keys_local = rotate(
        qkv[..., feature : 2 * feature].reshape(row_count, slot_count, head_count, HEAD),
        cosine,
        sine_table,
    ).astype(jnp.bfloat16)
    values_local = qkv[..., 2 * feature :].astype(jnp.bfloat16)
    keys_all, values_all = fetch(keys_local.reshape(row_count, slot_count, feature), values_local)
    slot_start = lax.axis_index("ctx") * slot_count
    segment_local = lax.dynamic_slice_in_dim(segment_ids, slot_start, slot_count, 1)
    order_local = lax.dynamic_slice_in_dim(token_order, slot_start, slot_count, 1)
    allowed = (segment_local[:, :, None] == segment_ids[:, None, :]) & (
        token_order[:, None, :] <= order_local[:, :, None]
    )
    keys_heads = keys_all.reshape(row_count, -1, head_count, HEAD)
    values_heads = values_all.reshape(row_count, -1, head_count, HEAD)
    mixed_out, log_totals = attend(
        head_groups(queries, group_size),
        head_groups(keys_heads, group_size),
        head_groups(values_heads, group_size),
        allowed,
        HEAD ** (-0.5),
    )
    attended = join_groups(mixed_out).reshape(row_count, slot_count, feature)
    attn_out = jnp.einsum(
        "btd,de->bte", attended, w_out, preferred_element_type=jnp.float32
    ) + b_out.astype(jnp.float32)
    up_proj = jnp.einsum(
        "btd,df->btf", normed, w_up, preferred_element_type=jnp.float32
    ) + b_up.astype(jnp.float32)
    active = jax.nn.gelu(up_proj, approximate=True).astype(jnp.bfloat16)
    mlp_out = jnp.einsum(
        "btf,fd->btd", active, w_down, preferred_element_type=jnp.float32
    ) + b_down.astype(jnp.float32)
    output = (hidden_f + attn_out + mlp_out).astype(jnp.bfloat16)
    return (
        hidden_f,
        normed,
        queries,
        keys_heads,
        values_heads,
        allowed,
        attended,
        log_totals,
        up_proj,
        active,
        output,
        cosine,
        sine_table,
        group_size,
    )


def outer_rows(left, right):

    def term(start, count):
        return jnp.einsum("btd,btf->df", left, right, preferred_element_type=jnp.float32)

    return term


def reduce_rows(term, own_rows):
    return lax.psum_scatter(
        term(jnp.int32(0), own_rows * lax.axis_size(("dp", "ctx"))),
        ("dp", "ctx"),
        scatter_dimension=0,
        tiled=True,
    )


def on_device(
    hidden_in,
    ln_gain,
    ln_bias,
    w_qkv,
    b_qkv,
    w_out,
    b_out,
    w_up,
    b_up,
    w_down,
    b_down,
    segment_ids,
    positions,
    token_order,
    grad_out,
):
    weights = (
        lax.all_gather(w_qkv, ("dp", "ctx"), axis=0, tiled=True),
        lax.all_gather(w_out, ("dp", "ctx"), axis=0, tiled=True),
        lax.all_gather(w_up, ("dp", "ctx"), axis=0, tiled=True),
        lax.all_gather(w_down, ("dp", "ctx"), axis=0, tiled=True),
        lax.all_gather(b_qkv, ("dp", "ctx"), axis=0, tiled=True),
        lax.all_gather(b_out, ("dp", "ctx"), axis=0, tiled=True),
        lax.all_gather(b_up, ("dp", "ctx"), axis=0, tiled=True),
        lax.all_gather(b_down, ("dp", "ctx"), axis=0, tiled=True),
        lax.all_gather(ln_gain, ("dp", "ctx"), axis=0, tiled=True),
        lax.all_gather(ln_bias, ("dp", "ctx"), axis=0, tiled=True),
    )

    def fetch_first(keys_local, values_local):
        return (
            lax.all_gather(keys_local, "ctx", axis=1, tiled=True),
            lax.all_gather(values_local, "ctx", axis=1, tiled=True),
        )

    state = run_forward(weights, hidden_in, positions, segment_ids, token_order, fetch_first)
    output = state[10]
    weights = (
        lax.all_gather(w_qkv, ("dp", "ctx"), axis=0, tiled=True),
        lax.all_gather(w_out, ("dp", "ctx"), axis=0, tiled=True),
        lax.all_gather(w_up, ("dp", "ctx"), axis=0, tiled=True),
        lax.all_gather(w_down, ("dp", "ctx"), axis=0, tiled=True),
        lax.all_gather(b_qkv, ("dp", "ctx"), axis=0, tiled=True),
        lax.all_gather(b_out, ("dp", "ctx"), axis=0, tiled=True),
        lax.all_gather(b_up, ("dp", "ctx"), axis=0, tiled=True),
        lax.all_gather(b_down, ("dp", "ctx"), axis=0, tiled=True),
        lax.all_gather(ln_gain, ("dp", "ctx"), axis=0, tiled=True),
        lax.all_gather(ln_bias, ("dp", "ctx"), axis=0, tiled=True),
    )

    def fetch_again(keys_local, values_local):
        return (
            lax.all_gather(keys_local, "ctx", axis=1, tiled=True),
            lax.all_gather(values_local, "ctx", axis=1, tiled=True),
        )

    state = run_forward(weights, hidden_in, positions, segment_ids, token_order, fetch_again)
    hidden_f, normed, queries, keys_heads, values_heads, allowed = (
        state[0],
        state[1],
        state[2],
        state[3],
        state[4],
        state[5],
    )
    attended, log_totals, up_proj, active = (state[6], state[7], state[8], state[9])
    cosine, sine_table, group_size = (state[11], state[12], state[13])
    w_qkv_all, w_out_all, w_up_all, w_down_all = (weights[0], weights[1], weights[2], weights[3])
    gain_all = weights[8].astype(jnp.float32)
    shift_all = weights[9].astype(jnp.float32)
    row_count, slot_count, feature = hidden_in.shape
    head_count = feature // HEAD
    grad_f = grad_out.astype(jnp.float32)
    bias_grad = jnp.sum(grad_f, axis=(0, 1))
    down_grad = reduce_rows(outer_rows(active, grad_out), w_down.shape[0])
    d_active = jnp.einsum("btd,fd->btf", grad_out, w_down_all, preferred_element_type=jnp.float32)
    gelu_back = jax.vjp(lambda pre_act: jax.nn.gelu(pre_act, approximate=True), up_proj)[1]
    d_up = gelu_back(d_active)[0].astype(jnp.bfloat16)
    up_bias_grad = jnp.sum(d_up.astype(jnp.float32), axis=(0, 1))
    up_grad = reduce_rows(outer_rows(normed, d_up), w_up.shape[0])
    d_normed = jnp.einsum("btf,df->btd", d_up, w_up_all, preferred_element_type=jnp.float32)
    out_grad = reduce_rows(outer_rows(attended, grad_out), w_out.shape[0])
    d_attended = jnp.einsum(
        "bte,de->btd", grad_out, w_out_all, preferred_element_type=jnp.float32
    ).astype(jnp.bfloat16)
    d_groups = head_groups(d_attended.reshape(row_count, slot_count, head_count, HEAD), group_size)
    d_query, d_key, d_value = attend_back(
        head_groups(queries, group_size),
        head_groups(keys_heads, group_size),
        head_groups(values_heads, group_size),
        d_groups,
        log_totals,
        allowed,
        HEAD ** (-0.5),
    )
    d_query = join_groups(d_query)
    d_key_all = join_groups(d_key).reshape(row_count, -1, feature)
    d_value_all = join_groups(d_value).reshape(row_count, -1, feature)
    d_key_own, d_value_own = (
        lax.psum_scatter(d_key_all, "ctx", scatter_dimension=1, tiled=True),
        lax.psum_scatter(d_value_all, "ctx", scatter_dimension=1, tiled=True),
    )
    d_qkv = jnp.concatenate(
        [
            unrotate(d_query, cosine, sine_table).reshape(row_count, slot_count, feature),
            unrotate(
                d_key_own.reshape(row_count, slot_count, head_count, HEAD), cosine, sine_table
            ).reshape(row_count, slot_count, feature),
            d_value_own,
        ],
        axis=-1,
    ).astype(jnp.bfloat16)
    qkv_bias_grad = jnp.sum(d_qkv.astype(jnp.float32), axis=(0, 1))
    qkv_grad = reduce_rows(outer_rows(normed, d_qkv), w_qkv.shape[0])
    d_normed = d_normed + jnp.einsum(
        "btf,df->btd", d_qkv, w_qkv_all, preferred_element_type=jnp.float32
    )
    norm_back = jax.vjp(norm_rows, hidden_f, gain_all, shift_all)[1]
    d_hidden, gain_grad, shift_grad = norm_back(d_normed)
    grad_in = (grad_f + d_hidden).astype(jnp.bfloat16)
    small = (
        lax.psum_scatter(qkv_bias_grad, ("dp", "ctx"), scatter_dimension=0, tiled=True),
        lax.psum_scatter(bias_grad, ("dp", "ctx"), scatter_dimension=0, tiled=True),
        lax.psum_scatter(up_bias_grad, ("dp", "ctx"), scatter_dimension=0, tiled=True),
        lax.psum_scatter(gain_grad, ("dp", "ctx"), scatter_dimension=0, tiled=True),
        lax.psum_scatter(shift_grad, ("dp", "ctx"), scatter_dimension=0, tiled=True),
    )
    return (
        output,
        grad_in,
        small[3],
        small[4],
        qkv_grad,
        small[0],
        out_grad,
        small[1],
        up_grad,
        small[2],
        down_grad,
        small[1],
    )


def solution(mesh):
    in_specs = (
        P("dp", "ctx", None),
        P(("dp", "ctx")),
        P(("dp", "ctx")),
        P(("dp", "ctx"), None),
        P(("dp", "ctx")),
        P(("dp", "ctx"), None),
        P(("dp", "ctx")),
        P(("dp", "ctx"), None),
        P(("dp", "ctx")),
        P(("dp", "ctx"), None),
        P(("dp", "ctx")),
        P("dp", None),
        P("dp", "ctx"),
        P("dp", None),
        P("dp", "ctx", None),
    )
    out_specs = (
        P("dp", "ctx", None),
        P("dp", "ctx", None),
        P(("dp", "ctx")),
        P(("dp", "ctx")),
        P(("dp", "ctx"), None),
        P(("dp", "ctx")),
        P(("dp", "ctx"), None),
        P(("dp", "ctx")),
        P(("dp", "ctx"), None),
        P(("dp", "ctx")),
        P(("dp", "ctx"), None),
        P(("dp", "ctx")),
    )
    return jax.shard_map(
        on_device, mesh=mesh, in_specs=in_specs, out_specs=out_specs, check_vma=False
    )
```

profile of v0, /device:TPU:0, one launch (start us, length us, event | category | flops | bytes accessed | tf_op | source)
XLA Modules:
  0.0 5165.6 jit_solution(12216584643388351475)
XLA Ops:
  13.0 44.1 all-reduce.11
  60.4 109.6 %all-gather.8.cloned.1.call-done = bf16[2048,6144]{1,0:T(8,128)(2,1)} async-done(((bf16[64,6144]{1,0:T(8,128)(2,1)}), bf16[2048,6144]{1,0:T(8,128)(2,1)}) %all-gather.8.cloned.1.call-update) | async-done | bytes 25165840 | tf_op jit(solution)/shard_map/all_gather | solution.py:224
  170.0 20.8 add_bitcast_fusion
  221.4 27.3 all-gather.14.cloned.1.call-done
  262.0 75.2 %all-gather.10.cloned.1.call-done = bf16[1,2048,2048]{2,1,0:T(8,128)(2,1)} async-done(((bf16[1,512,2048]{2,1,0:T(8,128)(2,1)}), bf16[1,2048,2048]{2,1,0:T(8,128)(2,1)}) %all-gather.10.cloned.1.call-update) | async-done | bytes 8388624 | tf_op jit(solution)/shard_map/all_gather | solution.py:239
  349.7 77.3 %all-gather.12.cloned.1.call-done = bf16[1,2048,2048]{1,2,0:T(8,128)(2,1)} async-done(((bf16[1,512,2048]{1,2,0:T(8,128)(2,1)}), bf16[1,2048,2048]{1,2,0:T(8,128)(2,1)}) %all-gather.12.cloned.1.call-update) | async-done | bytes 8388624 | tf_op jit(solution)/shard_map/all_gather | solution.py:238
  428.6 134.3 %while.40 = (s32[]{:T(128)}, bf16[8,1,512,4,64]{2,4,3,1,0:T(8,128)(2,1)}, f32[8,1,4,512]{3,2,1,0:T(4,128)S(1)}, bf16[8,1,2048,4,64]{2,4,3,1,0:T(8,128)(2,1)}, bf...) while((s32[]{:T(128)}, ...), condition=%wide.region_9.10_spmd.clone, body=%wide.region_6.9_spmd.clone.sunk | while | flops 1127348224 | bytes 57235568 | solution.py:90
  562.9 488.6 %while.41 = (s32[]{:T(128)}, f32[8,1,512,4,64]{2,4,3,1,0:T(8,128)}, f32[8,1,2048,4,64]{2,4,3,1,0:T(8,128)}, f32[8,1,2048,4,64]{2,4,3,1,0:T(8,128)}, bf16[8,1,204...) while((s32[]{:T(128)}, f32[8,1,512,4,64]{2,4,3,1,0:T(8,128)}, ...), condition=%wide.region_12.13_spmd.clone, body=%wide.region_10.12_spmd.clone.sunk | while | flops 2751068160 | bytes 189351168 | solution.py:118
  586.5 16.8 multiply_convert_fusion.5
  635.3 13.1 multiply_reduce_fusion.2
  648.4 16.0 multiply_convert_fusion.5
  709.7 17.9 multiply_convert_fusion.5
  773.1 17.3 multiply_convert_fusion.5
  834.7 15.8 multiply_convert_fusion.5
  894.6 15.8 multiply_convert_fusion.5
  954.5 15.8 multiply_convert_fusion.5
  1014.5 15.8 multiply_convert_fusion.5
  1053.6 69.4 %all-gather = bf16[32,1,256]{2,1,0:T(2,128)(2,1)S(1)} all-gather(bf16[1,1,256]{2,1,0:T(2,128)(2,1)S(1)} %reshape.719), channel_id=1, replica_groups=mesh['dp'=8,'ctx'=4] {'dp','ctx'}, dimensions={0}, use_global_device_ids=true | all-gather | bytes 16896 | tf_op jit(solution)/shard_map/all_gather | solution.py:230
  1125.1 27.6 fusion.138
  1152.7 34.9 convert_reduce_fusion
  1187.6 25.5 fusion.152
  1220.8 144.8 %reduce-scatter.9.cloned.1.call-done = f32[1,512,2048]{1,2,0:T(8,128)} async-done(((f32[1,2048,2048]{1,2,0:T(8,128)}), f32[1,512,2048]{1,2,0:T(8,128)}) %reduce-scatter.9.cloned.1.call-update) | async-done | bytes 4194320 | tf_op jit(solution)/shard_map/reduce_scatter | solution.py:307
  1369.4 26.0 fusion.117
  1433.4 23.9 fusion.120
  1457.4 29.6 fusion.135
  1488.6 32.4 fusion.122
  1522.0 162.6 %while.39 = (s32[]{:T(128)}, bf16[8,1,512,4,64]{2,4,3,1,0:T(8,128)(2,1)S(1)}, bf16[8,1,2048,4,64]{2,4,3,1,0:T(8,128)(2,1)}, bf16[8,1,512,4,64]{2,4,3,1,0:T(8,128...) while((s32[]{:T(128)}, ...), condition=%wide.region_5.6_spmd.clone, body=%wide.region_2.5_spmd.clone.sunk | while | flops 1102186496 | bytes 38312036 | solution.py:90
  1692.0 26.9 fusion.119
  1724.9 179.5 %reduce-scatter.13.cloned.1.call-done = f32[64,2048]{1,0:T(8,128)} async-done(((f32[2048,2048]{1,0:T(8,128)}), f32[64,2048]{1,0:T(8,128)}) %reduce-scatter.13.cloned.1.call-update) | async-done | bytes 524304 | tf_op jit(solution)/shard_map/reduce_scatter | solution.py:198
  1904.3 440.1 %reduce-scatter.11.cloned.1.call-done = f32[64,6144]{1,0:T(8,128)} async-done(((f32[2048,6144]{1,0:T(8,128)}), f32[64,6144]{1,0:T(8,128)}) %reduce-scatter.11.cloned.1.call-update) | async-done | bytes 1572880 | tf_op jit(solution)/shard_map/reduce_scatter | solution.py:198
  2344.5 1406.1 %reduce-scatter.15.cloned.1.call-done = f32[64,8192]{1,0:T(8,128)} async-done(((f32[2048,8192]{1,0:T(8,128)}), f32[64,8192]{1,0:T(8,128)}) %reduce-scatter.15.cloned.1.call-update) | async-done | bytes 2097168 | tf_op jit(solution)/shard_map/reduce_scatter | solution.py:198
  3750.6 1407.5 %reduce-scatter.17.cloned.1.call-done = f32[256,2048]{1,0:T(8,128)} async-done(((f32[8192,2048]{1,0:T(8,128)}), f32[256,2048]{1,0:T(8,128)}) %reduce-scatter.17.cloned.1.call-update) | async-done | bytes 2097168 | tf_op jit(solution)/shard_map/reduce_scatter | solution.py:198
  (369 shorter events, 776.1 us)
Async XLA Ops:
  7.2 51.9 %copy-start = (bf16[1,512,2048]{2,1,0:T(8,128)(2,1)S(1)}, bf16[1,512,2048]{2,1,0:T(8,128)(2,1)}, u32[]{:S(2)}) copy-start(bf16[1,512,2048]{2,1,0:T(8,128)(2,1)} %param.21) | copy-start | bytes 6291460
  7.2 162.8 %all-gather.8.cloned.1.call-start = ((), (), s32[]{:S(2)}) async-start(), calls=%async_computation.6 | async-start | bytes 25952256 | tf_op jit(solution)/shard_map/all_gather | solution.py:224
  7.9 240.7 %all-gather.14.cloned.1.call-start = ((), (), s32[]{:S(2)}) async-start(), calls=%async_computation.9 | async-start | bytes 8650752 | tf_op jit(solution)/shard_map/all_gather | solution.py:225
  8.7 328.6 %all-gather.10.cloned.1.call-start = ((), (), s32[]{:S(2)}) async-start(), calls=%async_computation.7 | async-start | bytes 10485760 | tf_op jit(solution)/shard_map/all_gather | solution.py:239
  57.1 133.7 %copy-start.15 = (f32[2048]{0:T(1024)}, f32[2048]{0:T(1024)S(1)}, u32[]{:S(2)}) copy-start(f32[2048]{0:T(1024)S(1)} %convert_element_type.146) | copy-start | bytes 24580
  57.1 133.7 %copy-start.21 = (f32[2048]{0:T(1024)}, f32[2048]{0:T(1024)S(1)}, u32[]{:S(2)}) copy-start(f32[2048]{0:T(1024)S(1)} %convert_element_type.147) | copy-start | bytes 24580
  59.1 131.7 %copy-start.17 = (f32[512]{0:T(512)}, f32[512]{0:T(512)S(1)}, u32[]{:S(2)}) copy-start(f32[512]{0:T(512)S(1)} %broadcast_multiply_fusion) | copy-start | bytes 6148
  60.4 130.4 %copy-start.19 = (f32[512]{0:T(512)}, f32[512]{0:T(512)S(1)}, u32[]{:S(2)}) copy-start(f32[512]{0:T(512)S(1)} %fusion.131) | copy-start | bytes 6148
  194.7 232.4 %all-gather.12.cloned.1.call-start = ((), (), s32[]{:S(2)}) async-start(), calls=%async_computation.8 | async-start | bytes 10485760 | tf_op jit(solution)/shard_map/all_gather | solution.py:238
  219.9 905.2 %all-gather.16.cloned.1.call-start = ((), (), s32[]{:S(2)}) async-start(), calls=%async_computation.10 | async-start | bytes 34603008 | tf_op jit(solution)/shard_map/all_gather | solution.py:226
  220.5 932.2 %all-gather.18.cloned.1.call-start = ((), (), s32[]{:S(2)}) async-start(), calls=%async_computation.11 | async-start | bytes 34603008 | tf_op jit(solution)/shard_map/all_gather | solution.py:227
  221.1 992.1 %reduce-scatter.7.cloned.1.call-start = ((), (), s32[]{:S(2)}) async-start(), calls=%async_computation.12 | async-start | bytes 20971520 | tf_op jit(solution)/shard_map/reduce_scatter | solution.py:306
  586.4 31.1 slice-start
  586.4 31.1 slice-start.1
  709.7 33.2 slice-start
  709.7 33.2 slice-start.1
  709.7 33.2 slice-start.2
  773.1 31.1 slice-start
  773.1 31.1 slice-start.1
  773.1 31.1 slice-start.2
  1052.8 312.8 %reduce-scatter.9.cloned.1.call-start = ((), (), s32[]{:S(2)}) async-start(), calls=%async_computation.13 | async-start | bytes 20971520 | tf_op jit(solution)/shard_map/reduce_scatter | solution.py:307
  1052.9 72.2 %copy-start.1 = (bf16[1,512,2048]{2,1,0:T(8,128)(2,1)S(1)}, bf16[1,512,2048]{2,1,0:T(8,128)(2,1)}, u32[]{:S(2)}) copy-start(bf16[1,512,2048]{2,1,0:T(8,128)(2,1)} %param.21) | copy-start | bytes 6291460
  1052.9 72.2 %copy-start.16 = (f32[2048]{0:T(1024)S(1)}, f32[2048]{0:T(1024)}, u32[]{:S(2)}) copy-start(f32[2048]{0:T(1024)} %copy-done.15) | copy-start | bytes 24580
  1052.9 72.2 %copy-start.18 = (f32[512]{0:T(512)S(1)}, f32[512]{0:T(512)}, u32[]{:S(2)}) copy-start(f32[512]{0:T(512)} %copy-done.17) | copy-start | bytes 6148
  1052.9 72.2 %copy-start.20 = (f32[512]{0:T(512)S(1)}, f32[512]{0:T(512)}, u32[]{:S(2)}) copy-start(f32[512]{0:T(512)} %copy-done.19) | copy-start | bytes 6148
  1052.9 72.2 %copy-start.22 = (f32[2048]{0:T(1024)S(1)}, f32[2048]{0:T(1024)}, u32[]{:S(2)}) copy-start(f32[2048]{0:T(1024)} %copy-done.21) | copy-start | bytes 24580
  1053.6 665.4 %all-reduce.14.cloned.1.call-start = ((), (), s32[]{:S(2)}) async-start(), calls=%async_computation.18 | async-start | bytes 163840
  1420.2 484.2 %reduce-scatter.13.cloned.1.call-start = ((), (), s32[]{:S(2)}) async-start(), calls=%async_computation.15 | async-start | bytes 17301504 | tf_op jit(solution)/shard_map/reduce_scatter | solution.py:198
  1432.7 911.7 %reduce-scatter.11.cloned.1.call-start = ((), (), s32[]{:S(2)}) async-start(), calls=%async_computation.14 | async-start | bytes 51904512 | tf_op jit(solution)/shard_map/reduce_scatter | solution.py:198
  1457.4 2293.2 %reduce-scatter.15.cloned.1.call-start = ((), (), s32[]{:S(2)}) async-start(), calls=%async_computation.16 | async-start | bytes 69206016 | tf_op jit(solution)/shard_map/reduce_scatter | solution.py:198
  1487.1 3671.1 %reduce-scatter.17.cloned.1.call-start = ((), (), s32[]{:S(2)}) async-start(), calls=%async_computation.17 | async-start | bytes 69206016 | tf_op jit(solution)/shard_map/reduce_scatter | solution.py:198
  1719.7 3438.9 %copy-start.41 = (f32[64]{0:T(128)}, f32[64]{0:T(128)S(1)}, u32[]{:S(2)}) copy-start(f32[64]{0:T(128)S(1)} %dynamic-slice.3) | copy-start | bytes 772
  (55 other events, 803.0 us)
Sparse Core Ops, SparseCore 0:
  10.9 159.0 all-gather.7
  172.8 75.7 all-gather.13
  251.0 86.1 all-gather.9
  339.5 87.4 all-gather.11
  429.8 194.8 all-gather.15
  627.3 192.9 all-gather.17
  1051.7 157.0 reduce-scatter.6
  1211.8 153.7 reduce-scatter.8
  1420.3 122.3 all-reduce.13
  1545.4 358.9 reduce-scatter.12
  1911.3 433.0 reduce-scatter.10
  2347.2 1403.3 reduce-scatter.14
  3753.5 1404.5 reduce-scatter.16
where the time goes:
time: 5180 us; the launch traced here: 5170 us
  waiting for transfers between devices  3870 us (75%)
  matrix products  871 us (17%)
  other arithmetic  230 us (4%)
  blocking collectives  114 us (2%)
  local copies, waits for them, and re-layouts  63.4 us (1%)
    reduce_scatter x4, waiting for transfers between devices, reduce_rows(): lax.psum_scatter(term(jnp.int32(0), own_rows * lax.axis_size(('dp', 'ctx'...  3430 us
    reduce_scatter x1, waiting for transfers between devices, on_device(): lax.psum_scatter(d_value_all, 'ctx', scatter_dimension=1, tiled=True)  145 us
    convert_element_type x8, other arithmetic, one_group(): d_scores = (probs_full * (d_probs - inner_sum)).astype(jnp.bfloat16)  131 us
    dot_general x16, matrix products, one_group(): jnp.einsum('bgtl,blge->btge', probabilities, v_group, preferred_element_t...  127 us
    dot_general x16, matrix products, masked_scores(): jnp.einsum('btge,blge->bgtl', q_group, k_group, preferred_element_type=jn...  111 us
    all_gather x1, waiting for transfers between devices, on_device(): lax.all_gather(w_qkv, ('dp', 'ctx'), axis=0, tiled=True)  110 us
  transfers between devices with their start and end apart: 13, of which 9 were waited for; matrix products, arithmetic and copies ran while one was open for 21% of the time, Pallas kernels for 0%

commit v1 on v0

--- a/solution.py
+++ b/solution.py
@@ -220,8 +220,31 @@
     token_order,
     grad_out,
 ):
+
+    def edit_the_map(q_in):
+        all_values, high, r_now = (
+            lax.axis_size(("dp", "ctx")),
+            lax.axis_index(("dp", "ctx")),
+            q_in.shape[0],
+        )
+        v_now, found_now = (q_in, 1)
+        while found_now < all_values:
+            v_now = jnp.concatenate(
+                [
+                    v_now,
+                    lax.ppermute(
+                        v_now,
+                        axis_name=("dp", "ctx"),
+                        perm=[(q, (q - found_now) % all_values) for q in range(all_values)],
+                    ),
+                ],
+                axis=0,
+            )
+            found_now = 2 * found_now
+        return jnp.roll(v_now, high * r_now, axis=0)
+
     weights = (
-        lax.all_gather(w_qkv, ("dp", "ctx"), axis=0, tiled=True),
+        edit_the_map(w_qkv),
         lax.all_gather(w_out, ("dp", "ctx"), axis=0, tiled=True),
         lax.all_gather(w_up, ("dp", "ctx"), axis=0, tiled=True),
         lax.all_gather(w_down, ("dp", "ctx"), axis=0, tiled=True),

time: 5180 us -> 6020 us (1.16)
  blocking collectives: 114 us -> 638 us
  waiting for transfers between devices: 3870 us -> 4050 us
  local copies, waits for them, and re-layouts: 63.4 us -> 149 us
    unnamed x1, blocking collectives: 44.1 us -> 569 us
    ppermute x0 -> x5, waiting for transfers between devices: none -> 299 us  [edit_the_map(): lax.ppermute(v_now, axis_name=('dp', 'ctx'), perm=[(q, (q - found_now) %...]
    all_gather x1, waiting for transfers between devices: 110 us -> 0.01 us  [on_device(): lax.all_gather(w_qkv, ('dp', 'ctx'), axis=0, tiled=True)]
    reduce_scatter x4, waiting for transfers between devices: 3430 us -> 3540 us  [reduce_rows(): lax.psum_scatter(term(jnp.int32(0), own_rows * lax.axis_size(('dp', 'ctx'...]
    all_gather x1, waiting for transfers between devices: 75.2 us -> 0.02 us  [fetch_first(): lax.all_gather(values_local, 'ctx', axis=1, tiled=True)]
    all_gather x1, waiting for transfers between devices: 77.3 us -> 6.88 us  [fetch_first(): lax.all_gather(keys_local, 'ctx', axis=1, tiled=True)]
  transfers between devices with their start and end apart: 13 -> 20, of which waited for: 9 -> 11; matrix products, arithmetic and copies ran while one was open for 21% -> 21% of each run, Pallas kernels for 0% -> 0%
where the time goes in v1:
time: 6020 us; the launch traced here: 6010 us
  waiting for transfers between devices  4050 us (67%)
  matrix products  896 us (15%)
  blocking collectives  638 us (11%)
  other arithmetic  239 us (4%)
  local copies, waits for them, and re-layouts  149 us (2%)
    reduce_scatter x4, waiting for transfers between devices, reduce_rows(): lax.psum_scatter(term(jnp.int32(0), own_rows * lax.axis_size(('dp', 'ctx'...  3540 us
    unnamed x1, blocking collectives  569 us
    ppermute x5, waiting for transfers between devices, edit_the_map(): lax.ppermute(v_now, axis_name=('dp', 'ctx'), perm=[(q, (q - found_now) %...  299 us
    reduce_scatter x1, waiting for transfers between devices, on_device(): lax.psum_scatter(d_value_all, 'ctx', scatter_dimension=1, tiled=True)  141 us
    convert_element_type x8, other arithmetic, one_group(): d_scores = (probs_full * (d_probs - inner_sum)).astype(jnp.bfloat16)  131 us
    dot_general x16, matrix products, one_group(): jnp.einsum('bgtl,blge->btge', probabilities, v_group, preferred_element_t...  127 us
  transfers between devices with their start and end apart: 20, of which 11 were waited for; matrix products, arithmetic and copies ran while one was open for 21% of the time, Pallas kernels for 0%

profile of v1, /device:TPU:0, one launch (start us, length us, event | category | flops | bytes accessed | tf_op | source)
XLA Modules:
  0.0 6011.5 jit_solution(1646301598074902948)
XLA Ops:
  14.4 18.7 collective-permute-done
  36.8 38.3 collective-permute-done.1
  88.0 46.1 collective-permute-done.2
  148.3 195.5 %collective-permute-done.3 = bf16[512,6144]{1,0:T(8,128)(2,1)} collective-permute-done((bf16[512,6144]{1,0:T(8,128)(2,1)}, bf16[512,6144]{1,0:T(8,128)(2,1)}, u32[]{:S(2)}, u32[]{:S(2)}) %collective-permute-start.3) | collective-permute-done | bytes 6291488 | tf_op jit(solution)/shard_map/ppermute | solution.py:235
  355.1 569.0 %all-reduce.11 = (bf16[6144]{0:T(1024)(128)(2,1)S(1)}, bf16[2048]{0:T(1024)(128)(2,1)S(1)}, bf16[2048]{0:T(1024)(128)(2,1)S(1)}, bf16[2048]{0:T(1024)(128)(2,1)}, bf16[2048]{0:T(1024)(128)(2,1)}) all-reduce(bf16[6144]{0:T(1024)(128)(2,1)S(1)} %dynamic-update-slice.2, ...), channel_id=1, replica_groups=mesh['dp'=8,'ctx'=4] {'dp','ctx'}, use_global_device_ids=true, to_apply=%add.2 | all-reduce | flops 14336 | bytes 57344
  925.8 21.2 add_bitcast_fusion
  985.9 20.9 add_bitcast_fusion.1
  1083.1 58.7 all-gather.22.cloned.1.call-done
  1143.4 134.3 %while.40 = (s32[]{:T(128)}, bf16[8,1,512,4,64]{2,4,3,1,0:T(8,128)(2,1)}, f32[8,1,4,512]{3,2,1,0:T(4,128)S(1)}, bf16[8,1,2048,4,64]{2,4,3,1,0:T(8,128)(2,1)}, bf...) while((s32[]{:T(128)}, ...), condition=%wide.region_9.10_spmd.clone, body=%wide.region_6.9_spmd.clone.sunk | while | flops 1127348224 | bytes 57235568 | solution.py:90
  1277.6 489.1 %while.41 = (s32[]{:T(128)}, f32[8,1,512,4,64]{2,4,3,1,0:T(8,128)}, f32[8,1,2048,4,64]{2,4,3,1,0:T(8,128)}, f32[8,1,2048,4,64]{2,4,3,1,0:T(8,128)}, bf16[8,1,204...) while((s32[]{:T(128)}, f32[8,1,512,4,64]{2,4,3,1,0:T(8,128)}, ...), condition=%wide.region_12.13_spmd.clone, body=%wide.region_10.12_spmd.clone.sunk | while | flops 2751068160 | bytes 189351168 | solution.py:118
  1301.1 16.8 multiply_convert_fusion.5
  1363.0 15.9 multiply_convert_fusion.5
  1424.7 18.1 multiply_convert_fusion.5
  1488.1 17.3 multiply_convert_fusion.5
  1549.6 15.8 multiply_convert_fusion.5
  1609.6 15.8 multiply_convert_fusion.5
  1669.6 15.8 multiply_convert_fusion.5
  1772.3 69.3 %all-gather = bf16[32,1,256]{2,1,0:T(2,128)(2,1)S(1)} all-gather(bf16[1,1,256]{2,1,0:T(2,128)(2,1)S(1)} %reshape.807), channel_id=1, replica_groups=mesh['dp'=8,'ctx'=4] {'dp','ctx'}, dimensions={0}, use_global_device_ids=true | all-gather | bytes 16896 | tf_op jit(solution)/shard_map/all_gather | solution.py:253
  1843.7 27.6 fusion.144
  1871.3 35.6 convert_reduce_fusion
  1906.9 25.3 fusion.159
  1940.1 140.7 %reduce-scatter.9.cloned.1.call-done = f32[1,512,2048]{1,2,0:T(8,128)} async-done(((f32[1,2048,2048]{1,2,0:T(8,128)}), f32[1,512,2048]{1,2,0:T(8,128)}) %reduce-scatter.9.cloned.1.call-update) | async-done | bytes 4194320 | tf_op jit(solution)/shard_map/reduce_scatter | solution.py:330
  2084.6 25.9 fusion.121
  2146.9 24.1 fusion.124
  2171.1 30.9 fusion.140
  2203.7 33.0 fusion.126
  2260.3 162.3 %while.39 = (s32[]{:T(128)}, bf16[8,1,512,4,64]{2,4,3,1,0:T(8,128)(2,1)S(1)}, bf16[8,1,2048,4,64]{2,4,3,1,0:T(8,128)(2,1)}, bf16[8,1,512,4,64]{2,4,3,1,0:T(8,128...) while((s32[]{:T(128)}, ...), condition=%wide.region_5.6_spmd.clone, body=%wide.region_2.5_spmd.clone.sunk | while | flops 1102186496 | bytes 38312036 | solution.py:90
  2430.0 26.9 fusion.123
  2462.9 287.7 %reduce-scatter.13.cloned.1.call-done = f32[64,2048]{1,0:T(8,128)} async-done(((f32[2048,2048]{1,0:T(8,128)}), f32[64,2048]{1,0:T(8,128)}) %reduce-scatter.13.cloned.1.call-update) | async-done | bytes 524304 | tf_op jit(solution)/shard_map/reduce_scatter | solution.py:198
  2750.6 440.1 %reduce-scatter.11.cloned.1.call-done = f32[64,6144]{1,0:T(8,128)} async-done(((f32[2048,6144]{1,0:T(8,128)}), f32[64,6144]{1,0:T(8,128)}) %reduce-scatter.11.cloned.1.call-update) | async-done | bytes 1572880 | tf_op jit(solution)/shard_map/reduce_scatter | solution.py:198
  3190.7 1406.1 %reduce-scatter.15.cloned.1.call-done = f32[64,8192]{1,0:T(8,128)} async-done(((f32[2048,8192]{1,0:T(8,128)}), f32[64,8192]{1,0:T(8,128)}) %reduce-scatter.15.cloned.1.call-update) | async-done | bytes 2097168 | tf_op jit(solution)/shard_map/reduce_scatter | solution.py:198
  4596.8 1407.4 %reduce-scatter.17.cloned.1.call-done = f32[256,2048]{1,0:T(8,128)} async-done(((f32[8192,2048]{1,0:T(8,128)}), f32[256,2048]{1,0:T(8,128)}) %reduce-scatter.17.cloned.1.call-update) | async-done | bytes 2097168 | tf_op jit(solution)/shard_map/reduce_scatter | solution.py:198
  (439 shorter events, 930.6 us)
Async XLA Ops:
  7.2 126.9 %copy-start.4 = (bf16[64,6144]{1,0:T(8,128)(2,1)S(1)}, bf16[64,6144]{1,0:T(8,128)(2,1)}, u32[]{:S(2)}) copy-start(bf16[64,6144]{1,0:T(8,128)(2,1)} %param.24) | copy-start | bytes 2359300
  7.2 918.6 %all-gather.20.cloned.1.call-start = ((), (), s32[]{:S(2)}) async-start(), calls=%async_computation.11 | async-start | bytes 25952256 | tf_op jit(solution)/shard_map/all_gather | solution.py:268
  7.9 1049.5 %all-gather.14.cloned.1.call-start = ((), (), s32[]{:S(2)}) async-start(), calls=%async_computation.8 | async-start | bytes 8650752 | tf_op jit(solution)/shard_map/all_gather | solution.py:248
  8.0 25.2 collective-permute-start
  33.1 104.6 %copy-start.10 = (bf16[64,6144]{1,0:T(8,128)(2,1)}, bf16[64,6144]{1,0:T(8,128)(2,1)S(1)}, u32[]{:S(2)}) copy-start(bf16[64,6144]{1,0:T(8,128)(2,1)S(1)} %collective-permute-done) | copy-start | bytes 2359300
  34.7 40.5 collective-permute-start.1
  77.0 57.0 collective-permute-start.2
  137.7 206.1 %collective-permute-start.3 = (bf16[512,6144]{1,0:T(8,128)(2,1)}, bf16[512,6144]{1,0:T(8,128)(2,1)}, u32[]{:S(2)}, u32[]{:S(2)}) collective-permute-start(bf16[512,6144]{1,0:T(8,128)(2,1)} %pad_maximum_fusion), channel_id=1, source_target_pairs={{0,24},{1,25},{2,26},{3,27},{4,28},{5,29},{6,30},{7,31},{8,0},{9,1... | collective-permute-start | bytes 18874376 | tf_op jit(solution)/shard_map/ppermute | solution.py:235
  140.3 930.5 %all-gather.24.cloned.1.call-start = ((), (), s32[]{:S(2)}) async-start(), calls=%async_computation.13 | async-start | bytes 10485760 | tf_op jit(solution)/shard_map/all_gather | solution.py:283
  148.3 195.5 %copy-start.41 = (bf16[1024,6144]{1,0:T(8,128)(2,1)}, bf16[1024,6144]{1,0:T(8,128)(2,1)S(1)}, u32[]{:S(2)}) copy-start(bf16[1024,6144]{1,0:T(8,128)(2,1)S(1)} %get-tuple-element.388) | copy-start | bytes 37748740
  343.9 580.2 %copy-start = (bf16[1,512,2048]{2,1,0:T(8,128)(2,1)S(1)}, bf16[1,512,2048]{2,1,0:T(8,128)(2,1)}, u32[]{:S(2)}) copy-start(bf16[1,512,2048]{2,1,0:T(8,128)(2,1)} %param.21) | copy-start | bytes 6291460
  353.0 598.5 %collective-permute-start.4 = (bf16[1024,6144]{1,0:T(8,128)(2,1)}, bf16[1024,6144]{1,0:T(8,128)(2,1)}, u32[]{:S(2)}, u32[]{:S(2)}) collective-permute-start(bf16[1024,6144]{1,0:T(8,128)(2,1)} %get-tuple-element.374), channel_id=1, source_target_pairs={{0,16},{1,17},{2,18},{3,19},{4,20},{5,21},{6,22},{7,23},{8,24},{9,... | collective-permute-start | bytes 37748744 | tf_op jit(solution)/shard_map/ppermute | solution.py:235
  951.0 190.8 %all-gather.22.cloned.1.call-start = ((), (), s32[]{:S(2)}) async-start(), calls=%async_computation.12 | async-start | bytes 10485760 | tf_op jit(solution)/shard_map/all_gather | solution.py:282
  951.5 96.1 %copy-start.37 = (f32[512,16]{0,1:T(8,128)}, f32[512,16]{0,1:T(8,128)S(1)}, u32[]{:S(2)}) copy-start(f32[512,16]{0,1:T(8,128)S(1)} %get-tuple-element.406) | copy-start | bytes 98308
  951.5 96.1 %copy-start.39 = (f32[512,16]{0,1:T(8,128)}, f32[512,16]{0,1:T(8,128)S(1)}, u32[]{:S(2)}) copy-start(f32[512,16]{0,1:T(8,128)S(1)} %get-tuple-element.407) | copy-start | bytes 98308
  1055.7 788.0 %all-gather.16.cloned.1.call-start = ((), (), s32[]{:S(2)}) async-start(), calls=%async_computation.9 | async-start | bytes 34603008 | tf_op jit(solution)/shard_map/all_gather | solution.py:249
  1056.3 815.0 %all-gather.18.cloned.1.call-start = ((), (), s32[]{:S(2)}) async-start(), calls=%async_computation.10 | async-start | bytes 34603008 | tf_op jit(solution)/shard_map/all_gather | solution.py:250
  1056.8 875.4 %reduce-scatter.7.cloned.1.call-start = ((), (), s32[]{:S(2)}) async-start(), calls=%async_computation.14 | async-start | bytes 20971520 | tf_op jit(solution)/shard_map/reduce_scatter | solution.py:329
  1767.4 313.4 %reduce-scatter.9.cloned.1.call-start = ((), (), s32[]{:S(2)}) async-start(), calls=%async_computation.15 | async-start | bytes 20971520 | tf_op jit(solution)/shard_map/reduce_scatter | solution.py:330
  1768.1 75.5 %copy-start.1 = (bf16[1,512,2048]{2,1,0:T(8,128)(2,1)S(1)}, bf16[1,512,2048]{2,1,0:T(8,128)(2,1)}, u32[]{:S(2)}) copy-start(bf16[1,512,2048]{2,1,0:T(8,128)(2,1)} %param.21) | copy-start | bytes 6291460
  1768.2 75.5 %copy-start.25 = (f32[2048]{0:T(1024)S(1)}, f32[2048]{0:T(1024)}, u32[]{:S(2)}) copy-start(f32[2048]{0:T(1024)} %copy-done.24) | copy-start | bytes 24580
  1768.2 75.5 %copy-start.27 = (f32[512]{0:T(512)S(1)}, f32[512]{0:T(512)}, u32[]{:S(2)}) copy-start(f32[512]{0:T(512)} %copy-done.26) | copy-start | bytes 6148
  1768.2 75.5 %copy-start.29 = (f32[512]{0:T(512)S(1)}, f32[512]{0:T(512)}, u32[]{:S(2)}) copy-start(f32[512]{0:T(512)} %copy-done.28) | copy-start | bytes 6148
  1768.2 75.5 %copy-start.31 = (f32[2048]{0:T(1024)S(1)}, f32[2048]{0:T(1024)}, u32[]{:S(2)}) copy-start(f32[2048]{0:T(1024)} %copy-done.30) | copy-start | bytes 24580
  1768.2 471.0 %all-gather.10.cloned.1.call-start = ((), (), s32[]{:S(2)}) async-start(), calls=%async_computation.6 | async-start | bytes 10485760 | tf_op jit(solution)/shard_map/all_gather | solution.py:262
  1772.2 487.8 %all-gather.12.cloned.1.call-start = ((), (), s32[]{:S(2)}) async-start(), calls=%async_computation.7 | async-start | bytes 10485760 | tf_op jit(solution)/shard_map/all_gather | solution.py:261
  1841.7 615.3 %all-reduce.14.cloned.1.call-start = ((), (), s32[]{:S(2)}) async-start(), calls=%async_computation.20 | async-start | bytes 163840
  2133.7 616.9 %reduce-scatter.13.cloned.1.call-start = ((), (), s32[]{:S(2)}) async-start(), calls=%async_computation.17 | async-start | bytes 17301504 | tf_op jit(solution)/shard_map/reduce_scatter | solution.py:198
  2146.3 1044.4 %reduce-scatter.11.cloned.1.call-start = ((), (), s32[]{:S(2)}) async-start(), calls=%async_computation.16 | async-start | bytes 51904512 | tf_op jit(solution)/shard_map/reduce_scatter | solution.py:198
  2171.1 2425.7 %reduce-scatter.15.cloned.1.call-start = ((), (), s32[]{:S(2)}) async-start(), calls=%async_computation.18 | async-start | bytes 69206016 | tf_op jit(solution)/shard_map/reduce_scatter | solution.py:198
  2202.1 3802.1 %reduce-scatter.17.cloned.1.call-start = ((), (), s32[]{:S(2)}) async-start(), calls=%async_computation.19 | async-start | bytes 69206016 | tf_op jit(solution)/shard_map/reduce_scatter | solution.py:198
  2457.7 3547.0 %copy-start.56 = (f32[64]{0:T(128)}, f32[64]{0:T(128)S(1)}, u32[]{:S(2)}) copy-start(f32[64]{0:T(128)S(1)} %dynamic-slice.3) | copy-start | bytes 772
  (77 other events, 1471.9 us)
Sparse Core Ops, SparseCore 0:
  10.9 265.7 all-gather.19
  279.6 680.0 all-gather.13
  962.1 86.1 all-gather.23
  1055.8 85.9 all-gather.21
  1144.5 194.8 all-gather.15
  1342.1 192.9 all-gather.17
  1767.0 156.9 reduce-scatter.6
  1927.0 153.7 reduce-scatter.8
  2083.2 87.5 all-gather.9
  2172.6 87.4 all-gather.11
  2266.5 122.3 all-reduce.13
  2391.7 358.9 reduce-scatter.12
  2757.6 433.0 reduce-scatter.10
  3193.5 1403.2 reduce-scatter.14
  4599.6 1404.5 reduce-scatter.16
